TPU v7x, 512 devices: a whole 4x4x16 slice. The times are simulated.
512 devices in a mesh: gx: 16 (over x, z_lo), gy: 8 (over y, core), ga: 4 (over z_hi).
Axes of the slice: x: 4, y: 4, z: 16 (z_hi: 4, z_lo: 4; z = z_hi * 4 + z_lo), core: 2. Of those that a mesh axis runs over, the one named last changes fastest.
Arguments:
- mixture_fields_initial: float32 [16, 256, 256, 128], P(None, 'gx', ('gy', 'ga')), may hold values from 0 to 1
- flow_speed_vector: float32 [3, 256, 256, 128], P(None, 'gx', ('gy', 'ga')), may hold values from -2 to 2
- thermal_field: float32 [256, 256, 128], P('gx', ('gy', 'ga')), may hold values from 1 to 3
- mass_diffusivity: float32 [16], replicated, may hold values from 0.05 to 0.3
- arrhenius_constant: float32 [16], replicated, may hold values from 0.3 to 3
- arrhenius_energy_temp: float32 [16], replicated, may hold values from 0.5 to 4
- production_coefficients: float32 [16, 16], replicated, may hold values from -1.5 to 1.5
- tucker_factor_east: float32 [256, 64], P('gx'), may hold values from -1 to 1, as said below
- tucker_factor_north: float32 [256, 64], P(('gy', 'ga')), may hold values from -1 to 1, as said below
- tucker_factor_vertical: float32 [128, 32], replicated, may hold values from -1 to 1, as said below
- tucker_factor_component: float32 [16, 8], replicated, may hold values from -1 to 1, as said below
Outputs:
- mixture_fields_final: float32 [16, 256, 256, 128], P(None, 'gx', ('gy', 'ga'))
- residual: float32 [16, 256, 256, 128], P(None, 'gx', ('gy', 'ga'))
- tucker_core: float32 [8, 64, 64, 32], P(None, 'gx', ('gy', 'ga'))
Inputs may be any that keep to these rules, and one draw needn't show every extreme that they name: tucker_factor_east has orthonormal columns. tucker_factor_north has orthonormal columns. tucker_factor_vertical has orthonormal columns. tucker_factor_component has orthonormal columns.
All inputs are finite; a program needn't handle non-finite values.
Results may differ from a plain program's by a relative error of at most 0.0001.
Values sent between devices are 32-bit elements; how exact they have to be, the bound alone decides.
A program may use at most 64 MiB of HBM per device.

v0:
```python
import jax
import jax.numpy as jnp
from jax import lax
from jax.sharding import PartitionSpec as P

SUB = 2


time_step = 0.5


def padded_2(block, sides, width):
    for axis, dim in sides:
        count = lax.axis_size(axis)
        forward = [(i, i + 1) for i in range(count - 1)]
        backward = [(target, source) for source, target in forward]
        low = lax.ppermute(
            lax.slice_in_dim(block, block.shape[dim] - width, None, axis=dim), axis, forward
        )
        high = lax.ppermute(lax.slice_in_dim(block, 0, width, axis=dim), axis, backward)
        block = jnp.concatenate([low, block, high], axis=dim)
    return block


def advance_solution(
    tensor_elements,
    flow_speed_vector,
    thermal_field,
    mass_diffusivity,
    arrhenius_constant,
    arrhenius_energy_temp,
    production_coefficients,
):
    padded = padded_2(tensor_elements, (("gx", 1), (("gy", "ga"), 2)), 1)
    x_plus = padded[:, 2:, 1:-1, :]
    x_minus = padded[:, :-2, 1:-1, :]
    y_plus = padded[:, 1:-1, 2:, :]
    y_minus = padded[:, 1:-1, :-2, :]
    zero_layer = jnp.zeros_like(tensor_elements[..., :1])
    z_plus = jnp.concatenate([tensor_elements[..., 1:], zero_layer], axis=3)
    z_minus = jnp.concatenate([zero_layer, tensor_elements[..., :-1]], axis=3)
    laplace = x_plus + x_minus + y_plus + y_minus + z_plus + z_minus - 6.0 * tensor_elements
    advect = 0.5 * (
        flow_speed_vector[0] * (x_plus - x_minus)
        + flow_speed_vector[1] * (y_plus - y_minus)
        + flow_speed_vector[2] * (z_plus - z_minus)
    )
    swap_neighbour_halo = jnp.concatenate([tensor_elements[1:], tensor_elements[:1]], axis=0)
    reaction_source_terms = (
        arrhenius_constant[:, None, None, None]
        * jnp.exp(-arrhenius_energy_temp[:, None, None, None] / thermal_field)
        * tensor_elements
        * swap_neighbour_halo
    )
    produced = jnp.einsum(
        "sk,kxyz->sxyz",
        production_coefficients,
        reaction_source_terms,
        precision=lax.Precision.HIGHEST,
    )
    return tensor_elements + time_step * (
        mass_diffusivity[:, None, None, None] * laplace - advect + produced
    )


def compress(
    mixture_snapshot_record,
    tucker_factor_east,
    tucker_factor_north,
    tucker_factor_vertical,
    tucker_factor_component,
):
    highest = lax.Precision.HIGHEST
    projected = jnp.einsum(
        "sxyz,sa->axyz", mixture_snapshot_record, tucker_factor_component, precision=highest
    )
    partial_value = jnp.einsum(
        "axyz,zd->axyd", projected, tucker_factor_vertical, precision=highest
    )
    partial_value = jnp.einsum(
        "axyd,yc->axcd", partial_value, tucker_factor_north, precision=highest
    )
    partial_value = lax.psum_scatter(partial_value, ("gy", "ga"), scatter_dimension=2, tiled=True)
    partial_value = jnp.einsum(
        "axcd,xb->abcd", partial_value, tucker_factor_east, precision=highest
    )
    core_block = lax.psum_scatter(partial_value, "gx", scatter_dimension=1, tiled=True)
    return core_block


def expand(
    core_block,
    tucker_factor_east,
    tucker_factor_north,
    tucker_factor_vertical,
    tucker_factor_component,
):
    highest = lax.Precision.HIGHEST
    columns = tucker_factor_east
    expanded = jnp.einsum(
        "abcd,xb->axcd",
        lax.all_gather(core_block, "gx", axis=1, tiled=True),
        columns,
        precision=highest,
    )
    columns = tucker_factor_north
    expanded = jnp.einsum(
        "axcd,yc->axyd",
        lax.all_gather(expanded, ("gy", "ga"), axis=2, tiled=True),
        columns,
        precision=highest,
    )
    expanded = jnp.einsum("axyd,zd->axyz", expanded, tucker_factor_vertical, precision=highest)
    return jnp.einsum("axyz,sa->sxyz", expanded, tucker_factor_component, precision=highest)


def body(
    mixture_fields_initial,
    flow_speed_vector,
    thermal_field,
    mass_diffusivity,
    arrhenius_constant,
    arrhenius_energy_temp,
    production_coefficients,
    tucker_factor_east,
    tucker_factor_north,
    tucker_factor_vertical,
    tucker_factor_component,
):
    mixture_snapshot_record = mixture_fields_initial
    for substep in range(SUB):
        mixture_snapshot_record = advance_solution(
            mixture_snapshot_record,
            flow_speed_vector,
            thermal_field,
            mass_diffusivity,
            arrhenius_constant,
            arrhenius_energy_temp,
            production_coefficients,
        )
    tucker_core = compress(
        mixture_snapshot_record,
        tucker_factor_east,
        tucker_factor_north,
        tucker_factor_vertical,
        tucker_factor_component,
    )
    residual = mixture_snapshot_record - expand(
        tucker_core,
        tucker_factor_east,
        tucker_factor_north,
        tucker_factor_vertical,
        tucker_factor_component,
    )
    mixture_fields_final = mixture_snapshot_record
    for substep in range(SUB):
        mixture_fields_final = advance_solution(
            mixture_fields_final,
            flow_speed_vector,
            thermal_field,
            mass_diffusivity,
            arrhenius_constant,
            arrhenius_energy_temp,
            production_coefficients,
        )
    return (mixture_fields_final, residual, tucker_core)


def solution(mesh):
    in_specs = (
        P(None, "gx", ("gy", "ga"), None),
        P(None, "gx", ("gy", "ga"), None),
        P("gx", ("gy", "ga"), None),
        P(),
        P(),
        P(),
        P(),
        P("gx", None),
        P(("gy", "ga"), None),
        P(),
        P(),
    )
    out_specs = (
        P(None, "gx", ("gy", "ga"), None),
        P(None, "gx", ("gy", "ga"), None),
        P(None, "gx", ("gy", "ga"), None),
    )
    return jax.shard_map(body, mesh=mesh, in_specs=in_specs, out_specs=out_specs, check_vma=False)
```

profile of v0, /device:TPU:1, one launch (start us, length us, event | category | flops | bytes accessed | tf_op | source)
XLA Modules:
  0.0 860.7 jit_solution(5794603200608948624)
XLA Ops:
  7.2 1.8 copy.56
  9.1 4.4 collective-permute-start.1
  17.0 2.4 collective-permute-done
  19.4 13.4 %collective-permute-start.2 = (f32[16,18,1,128]{3,0,2,1:T(8,128)S(1)}, f32[16,18,1,128]{3,0,2,1:T(8,128)S(1)}, u32[]{:S(2)}, u32[]{:S(2)}) collective-permute-start(f32[16,18,1,128]{3,0,2,1:T(8,128)S(1)} %get-tuple-element.18), channel_id=1, source_target_pairs={{1,0},{2,1},{3,2},{4,3},{5,4},{6,5},{7,6},{8,7},{9,8},{10,9},{11,1... | collective-permute-start | bytes 442376 | tf_op jit(solution)/shard_map/ppermute | solution.py:20
  32.7 1.9 collective-permute-start.3
  34.7 7.6 collective-permute-done.2
  42.3 5.5 collective-permute-done.3
  47.8 2.1 fusion.13
  51.2 4.2 collective-permute-start.5
  55.4 1.3 collective-permute-done.5
  56.8 5.9 collective-permute-start.6
  62.7 3.5 collective-permute-start.7
  66.7 7.9 collective-permute-done.7
  74.5 2.0 fusion.10
  77.8 3.5 convolution_bitcast_fusion
  81.3 3.1 copy.58
  86.4 521.4 %all-reduce.11.cloned.1.call-done = f32[8,16,64,32]{3,1,2,0:T(8,128)} async-done(((f32[8,16,64,32]{3,1,2,0:T(8,128)}), f32[8,16,64,32]{3,1,2,0:T(8,128)}) %all-reduce.11.cloned.1.call-update) | async-done | bytes 1048592
  607.8 1.5 convolution_bitcast_fusion.7
  611.8 4.0 collective-permute-start.9
  617.5 2.2 collective-permute-start.10
  619.7 7.0 collective-permute-start.11
  626.7 63.9 %reduce-scatter.5.cloned.1.call-done = f32[8,4,2,32]{3,0,2,1:T(8,128)} async-done(((f32[8,64,2,32]{3,0,2,1:T(8,128)}), f32[8,4,2,32]{3,0,2,1:T(8,128)}) %reduce-scatter.5.cloned.1.call-update) | async-done | bytes 8208 | tf_op jit(solution)/shard_map/reduce_scatter | solution.py:87
  690.6 39.9 %all_gather.6 = f32[8,64,2,32]{3,0,2,1:T(8,128)S(1)} all-gather(f32[8,4,2,32]{3,0,2,1:T(8,128)} %reduce-scatter.5.cloned.1.call-done), channel_id=1, replica_groups=mesh['gx'=16,'gy'=8,'ga'=4] {'gx'}, dimensions={1}, use_global_device_ids=true | all-gather | bytes 139264 | tf_op jit(solution)/shard_map/all_gather | solution.py:102
  732.2 2.0 fusion.7
  735.5 4.2 collective-permute-start.13
  740.8 24.7 %collective-permute-start.14 = (f32[16,18,1,128]{3,0,2,1:T(8,128)S(1)}, f32[16,18,1,128]{3,0,2,1:T(8,128)S(1)}, u32[]{:S(2)}, u32[]{:S(2)}) collective-permute-start(f32[16,18,1,128]{3,0,2,1:T(8,128)S(1)} %get-tuple-element.12), channel_id=1, source_target_pairs={{1,0},{2,1},{3,2},{4,3},{5,4},{6,5},{7,6},{8,7},{9,8},{10,9},{11,1... | collective-permute-start | bytes 442376 | tf_op jit(solution)/shard_map/ppermute | solution.py:20
  765.5 1.9 collective-permute-start.15
  767.9 4.5 collective-permute-done.14
  772.5 4.9 collective-permute-done.15
  777.3 2.0 fusion.4
  781.3 64.2 %all-gather.2.cloned.1.call-done = f32[8,16,64,32]{3,1,2,0:T(8,128)} async-done(((f32[8,16,2,32]{3,1,2,0:T(8,128)}), f32[8,16,64,32]{3,1,2,0:T(8,128)}) %all-gather.2.cloned.1.call-update) | async-done | bytes 1048592 | tf_op jit(solution)/shard_map/all_gather | solution.py:109
  845.5 5.5 fusion.15
  (79 shorter events, 21.7 us)
Async XLA Ops:
  7.2 70.1 %copy-start = (f32[128,32]{0,1:T(8,128)S(1)}, f32[128,32]{0,1:T(8,128)}, u32[]{:S(2)}) copy-start(f32[128,32]{0,1:T(8,128)} %param.20) | copy-start | bytes 49156
  7.2 600.7 %all-reduce.11.cloned.1.call-start = ((), (), s32[]{:S(2)}) async-start(), calls=%async_computation.3 | async-start | bytes 8388608
  9.1 6.7 collective-permute-start.1
  13.5 5.9 collective-permute-start
  15.1 0.7 copy-start.9
  15.1 1.2 copy-start.1
  15.1 19.5 %copy-start.2 = (f32[3,16,8,128]{3,2,1,0:T(8,128)S(1)}, f32[3,16,8,128]{3,2,1,0:T(8,128)}, u32[]{:S(2)}) copy-start(f32[3,16,8,128]{3,2,1,0:T(8,128)} %param.12) | copy-start | bytes 589828
  15.3 32.5 %slice-start = ((f32[16,16,8,128]{3,2,1,0:T(8,128)}), f32[1,16,8,128]{3,2,1,0:T(8,128)S(1)}, s32[]{:S(2)}) async-start(f32[16,16,8,128]{3,2,1,0:T(8,128)} %param.11), calls=%async_computation.4 | async-start | bytes 131072 | tf_op jit(solution)/shard_map/slice | solution.py:48
  15.3 32.5 %copy-start.7 = (f32[16,8,128]{2,1,0:T(8,128)S(1)}, f32[16,8,128]{2,1,0:T(8,128)}, u32[]{:S(2)}) copy-start(f32[16,8,128]{2,1,0:T(8,128)} %param.13) | copy-start | bytes 196612
  15.3 32.5 %copy-start.8 = (f32[16,16]{1,0:T(8,128)S(1)}, f32[16,16]{1,0:T(8,128)}, u32[]{:S(2)}) copy-start(f32[16,16]{1,0:T(8,128)} %param.17) | copy-start | bytes 3076
  15.3 32.5 %copy-start.10 = (f32[16]{0:T(128)S(1)}, f32[16]{0:T(128)}, u32[]{:S(2)}) copy-start(f32[16]{0:T(128)} %param.15) | copy-start | bytes 196
  15.3 32.5 %copy-start.11 = (f32[16]{0:T(128)S(1)}, f32[16]{0:T(128)}, u32[]{:S(2)}) copy-start(f32[16]{0:T(128)} %param.14) | copy-start | bytes 196
  19.4 22.9 %collective-permute-start.2 = (f32[16,18,1,128]{3,0,2,1:T(8,128)S(1)}, f32[16,18,1,128]{3,0,2,1:T(8,128)S(1)}, u32[]{:S(2)}, u32[]{:S(2)}) collective-permute-start(f32[16,18,1,128]{3,0,2,1:T(8,128)S(1)} %get-tuple-element.18), channel_id=1, source_target_pairs={{1,0},{2,1},{3,2},{4,3},{5,4},{6,5},{7,6},{8,7},{9,8},{10,9},{11,1... | collective-permute-start | bytes 442376 | tf_op jit(solution)/shard_map/ppermute | solution.py:20
  32.7 15.1 %collective-permute-start.3 = (f32[16,18,1,128]{3,0,2,1:T(8,128)S(1)}, f32[16,18,1,128]{3,0,2,1:T(8,128)S(1)}, u32[]{:S(2)}, u32[]{:S(2)}) collective-permute-start(f32[16,18,1,128]{3,0,2,1:T(8,128)S(1)} %get-tuple-element.19), channel_id=1, source_target_pairs={{0,1},{1,2},{2,3},{3,4},{4,5},{5,6},{6,7},{7,8},{8,9},{9,10},{10,1... | collective-permute-start | bytes 442376 | tf_op jit(solution)/shard_map/ppermute | solution.py:17
  49.9 5.5 collective-permute-start.4
  51.2 5.5 collective-permute-start.5
  56.8 9.9 %collective-permute-start.6 = (f32[16,18,1,128]{3,0,2,1:T(8,128)S(1)}, f32[16,18,1,128]{3,0,2,1:T(8,128)S(1)}, u32[]{:S(2)}, u32[]{:S(2)}) collective-permute-start(f32[16,18,1,128]{3,0,2,1:T(8,128)S(1)} %get-tuple-element.16), channel_id=1, source_target_pairs={{1,0},{2,1},{3,2},{4,3},{5,4},{6,5},{7,6},{8,7},{9,8},{10,9},{11,1... | collective-permute-start | bytes 442376 | tf_op jit(solution)/shard_map/ppermute | solution.py:20
  62.7 11.9 %collective-permute-start.7 = (f32[16,18,1,128]{3,0,2,1:T(8,128)S(1)}, f32[16,18,1,128]{3,0,2,1:T(8,128)S(1)}, u32[]{:S(2)}, u32[]{:S(2)}) collective-permute-start(f32[16,18,1,128]{3,0,2,1:T(8,128)S(1)} %get-tuple-element.17), channel_id=1, source_target_pairs={{0,1},{1,2},{2,3},{3,4},{4,5},{5,6},{6,7},{7,8},{8,9},{9,10},{10,1... | collective-permute-start | bytes 442376 | tf_op jit(solution)/shard_map/ppermute | solution.py:17
  74.5 2.0 copy-start.5
  76.6 1.3 copy-start.6
  84.4 523.4 %copy-start.4 = (f32[16,64]{1,0:T(8,128)S(1)}, f32[16,64]{1,0:T(8,128)}, u32[]{:S(2)}) copy-start(f32[16,64]{1,0:T(8,128)} %param.18) | copy-start | bytes 12292
  84.4 606.1 %reduce-scatter.5.cloned.1.call-start = ((), (), s32[]{:S(2)}) async-start(), calls=%async_computation.1 | async-start | bytes 557056 | tf_op jit(solution)/shard_map/reduce_scatter | solution.py:87
  610.4 235.1 %all-gather.2.cloned.1.call-start = ((), (), s32[]{:S(2)}) async-start(), calls=%async_computation.2 | async-start | bytes 4325376 | tf_op jit(solution)/shard_map/all_gather | solution.py:109
  610.5 5.9 collective-permute-start.8
  611.8 5.7 collective-permute-start.9
  617.5 114.7 %collective-permute-start.10 = (f32[16,18,1,128]{3,0,2,1:T(8,128)S(1)}, f32[16,18,1,128]{3,0,2,1:T(8,128)S(1)}, u32[]{:S(2)}, u32[]{:S(2)}) collective-permute-start(f32[16,18,1,128]{3,0,2,1:T(8,128)S(1)} %get-tuple-element.14), channel_id=1, source_target_pairs={{1,0},{2,1},{3,2},{4,3},{5,4},{6,5},{7,6},{8,7},{9,8},{10,9},{11,1... | collective-permute-start | bytes 442376 | tf_op jit(solution)/shard_map/ppermute | solution.py:20
  619.7 112.4 %collective-permute-start.11 = (f32[16,18,1,128]{3,0,2,1:T(8,128)S(1)}, f32[16,18,1,128]{3,0,2,1:T(8,128)S(1)}, u32[]{:S(2)}, u32[]{:S(2)}) collective-permute-start(f32[16,18,1,128]{3,0,2,1:T(8,128)S(1)} %get-tuple-element.15), channel_id=1, source_target_pairs={{0,1},{1,2},{2,3},{3,4},{4,5},{5,6},{6,7},{7,8},{8,9},{9,10},{10,1... | collective-permute-start | bytes 442376 | tf_op jit(solution)/shard_map/ppermute | solution.py:17
  734.2 5.5 collective-permute-start.12
  735.5 5.3 collective-permute-start.13
  740.8 31.7 %collective-permute-start.14 = (f32[16,18,1,128]{3,0,2,1:T(8,128)S(1)}, f32[16,18,1,128]{3,0,2,1:T(8,128)S(1)}, u32[]{:S(2)}, u32[]{:S(2)}) collective-permute-start(f32[16,18,1,128]{3,0,2,1:T(8,128)S(1)} %get-tuple-element.12), channel_id=1, source_target_pairs={{1,0},{2,1},{3,2},{4,3},{5,4},{6,5},{7,6},{8,7},{9,8},{10,9},{11,1... | collective-permute-start | bytes 442376 | tf_op jit(solution)/shard_map/ppermute | solution.py:20
  765.5 11.9 %collective-permute-start.15 = (f32[16,18,1,128]{3,0,2,1:T(8,128)S(1)}, f32[16,18,1,128]{3,0,2,1:T(8,128)S(1)}, u32[]{:S(2)}, u32[]{:S(2)}) collective-permute-start(f32[16,18,1,128]{3,0,2,1:T(8,128)S(1)} %get-tuple-element.13), channel_id=1, source_target_pairs={{0,1},{1,2},{2,3},{3,4},{4,5},{5,6},{6,7},{7,8},{8,9},{9,10},{10,1... | collective-permute-start | bytes 442376 | tf_op jit(solution)/shard_map/ppermute | solution.py:17
  779.4 1.3 copy-start.3
Sparse Core Ops, SparseCore 0:
  84.5 523.2 all-reduce.10
  611.2 79.3 reduce-scatter.4
  731.8 113.7 all-gather.1
where the time goes:
time: 861 us
  waiting for transfers between devices  686 us (80%)
  starting transfers between devices  82.5 us (10%)
  blocking collectives  39.9 us (5%)
  matrix products  22.9 us (3%)
  between operations  14.9 us (2%)
  local copies, waits for them, and re-layouts  14.2 us (2%)
    unnamed x4, waiting for transfers between devices  521 us
    all_gather x1, waiting for transfers between devices, expand(): lax.all_gather(expanded, ('gy', 'ga'), axis=2, tiled=True)  64.2 us
    reduce_scatter x1, waiting for transfers between devices, compress(): lax.psum_scatter(partial_value, 'gx', scatter_dimension=1, tiled=True)  63.9 us
    ppermute x8, starting transfers between devices, padded_2(): lax.ppermute(lax.slice_in_dim(block, 0, width, axis=dim), axis, backward)  51.3 us
    all_gather x1, blocking collectives, expand(): lax.all_gather(core_block, 'gx', axis=1, tiled=True)  39.9 us
    ppermute x8, starting transfers between devices, padded_2(): lax.ppermute(lax.slice_in_dim(block, block.shape[dim] - width, None, axis...  31 us
    ppermute x8, waiting for transfers between devices, padded_2(): lax.ppermute(lax.slice_in_dim(block, block.shape[dim] - width, None, axis...  21.7 us
  transfers between devices with their start and end apart: 19, of which 13 were waited for; matrix products, arithmetic and copies ran while one was open for 1% of the time, Pallas kernels for 0%

commit v1 on v0

v1 whole, which is shorter than its diff:
```python
import functools
import jax
import jax.numpy as jnp
from jax import lax
from jax.experimental import pallas as pl
from jax.experimental.pallas import tpu as pltpu
from jax.sharding import PartitionSpec as P

MESH = pl.DeviceIdType.MESH
HI = lax.Precision.HIGHEST
F32 = jnp.float32
SPECIES = 16
RANK_S = 8
NX = 16
NY = 8
NZ = 128
DX = 16
DY = 32
GA = 4
GY = 8
ZL = 4
CHUNKS = 4
CX = NX // CHUNKS
ORDER = (0, 3, 1, 2)


def dot(a, b):
    return lax.dot_general(a, b, (((1,), (0,)), ((), ())), precision=HI, preferred_element_type=F32)


def dot_tn(a, b):
    return lax.dot_general(a, b, (((0,), (0,)), ((), ())), precision=HI, preferred_element_type=F32)


def dot_nt(a, b):
    return lax.dot_general(a, b, (((1,), (1,)), ((), ())), precision=HI, preferred_element_type=F32)


def iota(shape, dim):
    return lax.broadcasted_iota(jnp.int32, shape, dim)


def kernel(
    v_hbm, flow_hbm, temp_hbm, diff_ref, pre_ref, energy_ref, prod_ref, comp_ref,
    east_ref, north_ref, vert_ref,
    final_hbm, resid_hbm, core_ref,
    V, F, T, K, PC, CC, HY, FY, S, VT, NF, EF,
    PB, G, QB, H, MB, Q8, UB, W, CS, CO, RES,
    load_sem, out_sem,
    sx, rx, sy, ry,
    sn1, rn1, sn2, rn2, se1, re1, se2, re2,
    sp, rp, sq, rq, sm, rm, su, ru, sc, rc,
):
    gx = lax.axis_index("gx")
    gy = lax.axis_index("gy")
    ga = lax.axis_index("ga")
    me = gy * GA + ga
    zl = lax.rem(gx, ZL)
    xh = gx // ZL

    def at_y(j):
        return {"gx": gx, "gy": j // GA, "ga": lax.rem(j, GA)}

    def at_x(m):
        return {"gx": m, "gy": gy, "ga": ga}

    barrier = pltpu.get_barrier_semaphore()

    def greet_y(k, c):
        pl.semaphore_signal(barrier, inc=1, device_id=at_y(lax.rem(me + k, DY)), device_id_type=MESH)
        return c

    def greet_x(k, c):
        pl.semaphore_signal(barrier, inc=1, device_id=at_x(lax.rem(gx + k, DX)), device_id_type=MESH)
        return c

    lax.fori_loop(1, DY, greet_y, 0)
    lax.fori_loop(1, DX, greet_x, 0)

    load_v = pltpu.make_async_copy(v_hbm, V.at[0, :, pl.ds(1, NX)], load_sem.at[0])
    load_f = pltpu.make_async_copy(flow_hbm, F, load_sem.at[1])
    load_t = pltpu.make_async_copy(temp_hbm, T, load_sem.at[2])
    load_v.start()
    load_f.start()
    load_t.start()

    zeros = jnp.zeros((SPECIES, NY, NZ), F32)
    zface = jnp.zeros((NX, SPECIES, NZ), F32)
    for n in range(4):
        @pl.when(gx == 0)
        def _():
            V[n, :, 0] = zeros

        @pl.when(gx == DX - 1)
        def _():
            V[n, :, NX + 1] = zeros

        @pl.when(me == 0)
        def _():
            HY[n, 0] = zface

        @pl.when(me == DY - 1)
        def _():
            HY[n, 1] = zface

    load_v.wait()

    def pack(x, c):
        for s in range(SPECIES):
            tile = V[0, s, x + 1]
            FY[0, 0, x, s:s + 1, :] = tile[0:1, :]
            FY[0, 1, x, s:s + 1, :] = tile[NY - 1:NY, :]
        return c

    lax.fori_loop(0, NX, pack, 0)
    pl.semaphore_wait(barrier, DY - 1 + DX - 1)

    def copy_x(n, up):
        return pltpu.make_async_remote_copy(
            src_ref=V.at[n, :, NX if up else 1],
            dst_ref=V.at[n, :, 0 if up else NX + 1],
            send_sem=sx.at[n, up],
            recv_sem=rx.at[n, up],
            device_id=at_x(gx + 1 if up else gx - 1),
            device_id_type=MESH,
        )

    def copy_y(n, up, c):
        part = pl.ds(c * CX, CX)
        return pltpu.make_async_remote_copy(
            src_ref=FY.at[n, up, part],
            dst_ref=HY.at[n, 1 - up, part],
            send_sem=sy.at[n, up, c],
            recv_sem=ry.at[n, up, c],
            device_id=at_y(me + 1 if up else me - 1),
            device_id_type=MESH,
        )

    def has(axis_up):
        axis, up = axis_up
        if axis == "x":
            return gx < DX - 1 if up else gx > 0
        return me < DY - 1 if up else me > 0

    def send_x(n, up):
        @pl.when(has(("x", up)))
        def _():
            copy_x(n, up).start()

    def send_y(n, c):
        for up in (0, 1):
            @pl.when(has(("y", up)))
            def _():
                copy_y(n, up, c).start()

    def recv_x(n, up):
        @pl.when(has(("x", 1 - up)))
        def _():
            copy_x(n, up).wait_recv()

    def recv_y(n, c):
        for up in (0, 1):
            @pl.when(has(("y", 1 - up)))
            def _():
                copy_y(n, up, c).wait_recv()

    send_x(0, 0)
    send_x(0, 1)
    for c in ORDER:
        send_y(0, c)

    old = iota((64, 128), 0)
    spread = (iota((64, 128), 1) == (old >> 2) * 8 + (old & 3)).astype(F32)
    NF[me] = dot(north_ref[...], spread)
    eye = (iota((64, 128), 1) == iota((64, 128), 0)).astype(F32)
    EF[gx] = dot(east_ref[...], eye)

    def n1(k):
        return pltpu.make_async_remote_copy(
            NF.at[me], NF.at[me], sn1, rn1,
            device_id=at_y(gy * GA + lax.rem(ga + k, GA)), device_id_type=MESH)

    def n2(k):
        part = pl.ds(gy * GA, GA)
        return pltpu.make_async_remote_copy(
            NF.at[part], NF.at[part], sn2, rn2,
            device_id=at_y(lax.rem(gy + k, GY) * GA + ga), device_id_type=MESH)

    def e1(k):
        return pltpu.make_async_remote_copy(
            EF.at[gx], EF.at[gx], se1, re1,
            device_id=at_x(xh * ZL + lax.rem(zl + k, ZL)), device_id_type=MESH)

    def e2(k):
        part = pl.ds(xh * ZL, ZL)
        return pltpu.make_async_remote_copy(
            EF.at[part], EF.at[part], se2, re2,
            device_id=at_x(lax.rem(xh + k, DX // ZL) * ZL + zl), device_id_type=MESH)

    for k in range(1, GA):
        n1(k).start()
    for k in range(1, ZL):
        e1(k).start()

    def taken(ref, send, recv):
        return pltpu.make_async_remote_copy(
            ref, ref, send, recv, device_id=at_y(lax.rem(me + 1, DY)), device_id_type=MESH)

    load_t.wait()
    load_f.wait()

    def rates(x, c):
        inverse = 1.0 / T[x]
        for k in range(SPECIES):
            K[k, x] = (0.5 * pre_ref[k]) * jnp.exp((-energy_ref[k]) * inverse)
        for d in range(3):
            F[d, x] = 0.25 * F[d, x]
        return c

    lax.fori_loop(0, NX, rates, 0)

    def splat(s, c):
        for k in range(SPECIES):
            PC[s * SPECIES + k] = jnp.full((8, 128), prod_ref[s, k], F32)
        for a in range(RANK_S):
            CC[s * RANK_S + a] = jnp.full((8, 128), comp_ref[s, a], F32)
        return c

    lax.fori_loop(0, SPECIES, splat, 0)

    spot = iota((32, 512), 1)
    pick = (iota((32, 512), 0) == (spot >> 7) * 8 + (spot & 7)).astype(F32)
    VT[...] = dot(vert_ref[...], pick)

    row = iota((NY, NZ), 0)
    lane = iota((NY, NZ), 1)

    def advance(n, x, last):
        vs = [V[n, s, x + 1] for s in range(SPECIES)]
        react = [K[k, x] * vs[k] * vs[(k + 1) % SPECIES] for k in range(SPECIES)]
        fx, fy, fz = F[0, x], F[1, x], F[2, x]
        for s in range(SPECIES):
            v = vs[s]
            xp, xm = V[n, s, x + 2], V[n, s, x]
            up = jnp.broadcast_to(HY[n, 1, x, s:s + 1, :], (NY, NZ))
            down = jnp.broadcast_to(HY[n, 0, x, s:s + 1, :], (NY, NZ))
            yp = jnp.where(row == NY - 1, up, pltpu.roll(v, NY - 1, 0))
            ym = jnp.where(row == 0, down, pltpu.roll(v, 1, 0))
            zp = jnp.where(lane == NZ - 1, 0.0, pltpu.roll(v, NZ - 1, 1))
            zm = jnp.where(lane == 0, 0.0, pltpu.roll(v, 1, 1))
            half = 0.5 * diff_ref[s]
            total = (1.0 - 6.0 * half) * v + half * ((xp + xm) + (yp + ym) + (zp + zm))
            total = total - (fx * (xp - xm) + fy * (yp - ym) + fz * (zp - zm))
            made = PC[s * SPECIES] * react[0]
            for k in range(1, SPECIES):
                made = made + PC[s * SPECIES + k] * react[k]
            total = total + made
            V[n + 1, s, x + 1] = total
            if not last:
                FY[n + 1, 0, x, s:s + 1, :] = total[0:1, :]
                FY[n + 1, 1, x, s:s + 1, :] = total[NY - 1:NY, :]

    def step(n, c):
        last = n == 3
        recv_y(n, c)
        if c == 0:
            recv_x(n, 1)
        if c == CHUNKS - 1:
            recv_x(n, 0)

        def body(i, carry):
            advance(n, c * CX + i, last)
            return carry

        lax.fori_loop(0, CX, body, 0)
        if not last:
            send_y(n + 1, c)
            if c == 0:
                send_x(n + 1, 0)
            if c == CHUNKS - 1:
                send_x(n + 1, 1)
        else:
            save(c).start()

    def save(c):
        return pltpu.make_async_copy(
            V.at[4, :, pl.ds(1 + c * CX, CX)],
            final_hbm.at[:, pl.ds(c * CX, CX)],
            out_sem.at[c])

    step(0, ORDER[0])
    taken(NF.at[pl.ds(0, GA - 1)], sn1, rn1).wait()
    for k in range(1, GY):
        n2(k).start()
    taken(EF.at[pl.ds(0, ZL - 1)], se1, re1).wait()
    for k in range(1, DX // ZL):
        e2(k).start()
    for c in ORDER[1:]:
        step(0, c)
    for c in ORDER:
        step(1, c)

    def squash(x, carry):
        vs = [V[2, s, x + 1] for s in range(SPECIES)]
        for a in range(RANK_S):
            total = CC[a] * vs[0]
            for s in range(1, SPECIES):
                total = total + CC[s * RANK_S + a] * vs[s]
            S[a, x] = total
        return carry

    lax.fori_loop(0, NX, squash, 0)
    wide = ((iota((NX, NY, 512), 2) & 127) >> 3) == iota((NX, NY, 512), 0)

    def project(a, carry):
        out = dot(S[a].reshape(NX * NY, NZ), VT[...]).reshape(NX, NY, 512)
        out = jnp.sum(jnp.where(wide, out, 0.0), axis=0)
        for d in range(4):
            PB[a * 4 + d] = out[:, d * 128:(d + 1) * 128]
        return carry

    lax.fori_loop(0, RANK_S, project, 0)

    def to_y(src, dst, send, recv):
        def go(k, carry):
            j = lax.rem(me + k, DY)
            pltpu.make_async_remote_copy(
                src.at[j], dst.at[me], send, recv, device_id=at_y(j), device_id_type=MESH).start()
            return carry
        lax.fori_loop(1, DY, go, 0)

    def to_x(src, dst, send, recv):
        def go(k, carry):
            m = lax.rem(gx + k, DX)
            pltpu.make_async_remote_copy(
                src.at[m], dst.at[gx], send, recv, device_id=at_x(m), device_id_type=MESH).start()
            return carry
        lax.fori_loop(1, DX, go, 0)

    def done_y(ref, send, recv):
        taken(ref.at[pl.ds(0, DY - 1)], send, recv).wait()

    def done_x(ref, send, recv):
        taken(ref.at[pl.ds(0, DX - 1)], send, recv).wait()

    to_y(PB, G, sp, rp)
    G[me] = PB[me]

    for c in ORDER:
        step(2, c)

    taken(NF.at[pl.ds(0, GA * (GY - 1))], sn2, rn2).wait()
    taken(EF.at[pl.ds(0, ZL * (DX // ZL - 1))], se2, re2).wait()
    done_y(G, sp, rp)
    north = NF[...].reshape(DY * NY, 128)
    QB[...] = dot_tn(north, G[...].reshape(DY * NY, 128)).reshape(DX, 8, 128)
    to_x(QB, H, sq, rq)
    H[gx] = QB[gx]

    step(3, ORDER[0])

    done_x(H, sq, rq)
    own_x = (iota((DX, NX, 128), 2) >> 3) == iota((DX, NX, 128), 1)
    blocks = []
    for c in range(4):
        spread_h = jnp.broadcast_to(H[:, c:c + 1, :], (DX, NX, 128))
        blocks.append(jnp.where(own_x, spread_h, 0.0).reshape(DX * NX, 128))
    east = EF[...].reshape(DX * NX, 128)
    core = dot_tn(east, jnp.concatenate(blocks, axis=1))
    piece = jnp.zeros((128, 128), F32)
    slot = iota((128, 128), 1) >> 3
    b_low = iota((128, 128), 0) & 3
    parts = []
    for c in range(4):
        part = core[:, c * 128:(c + 1) * 128]
        for shift in (64, 32, 16, 8):
            part = part + pltpu.roll(part, shift, 1)
        parts.append(part)
        piece = piece + jnp.where(slot == c * 4 + b_low, part, 0.0)
    out = dot(east, jnp.concatenate(parts, axis=1))
    for c in range(4):
        block = out[:, c * 128:(c + 1) * 128].reshape(DX, NX, 128)
        MB[:, c, :] = jnp.sum(jnp.where(own_x, block, 0.0), axis=1)
    MB[:, 4, :] = jnp.sum(piece[:64].reshape(DX, 4, 128), axis=1)
    for c in range(5, 8):
        MB[:, c, :] = jnp.zeros((DX, 128), F32)
    to_x(MB, Q8, sm, rm)
    Q8[gx] = MB[gx]

    step(3, ORDER[1])

    done_x(Q8, sm, rm)
    UB[...] = dot(NF[...].reshape(DY * NY, 128), Q8[...].reshape(DX * 8, 128)).reshape(DY, NY, 128)
    to_y(UB, W, su, ru)
    W[me] = UB[me]
    for m in range(DX):
        CS[m] = Q8[m, 4:5, :]
    own = CO.at[lax.rem(me, 4) * 8 + me // 4]

    def core_go(k, carry):
        j = lax.rem(me + k, DY)
        pltpu.make_async_remote_copy(
            CS.at[j // 2], own, sc, rc, device_id=at_y(j), device_id_type=MESH).start()
        return carry

    lax.fori_loop(1, DY, core_go, 0)
    CO[lax.rem(me, 4) * 8 + me // 4] = CS[me // 2]

    step(3, ORDER[2])
    step(3, ORDER[3])

    done_y(W, su, ru)
    tall = (iota((NX, NY, 128), 2) >> 3) == iota((NX, NY, 128), 0)

    def rebuild(a, carry):
        left = []
        for d in range(4):
            copies = jnp.broadcast_to(W[a * 4 + d][None], (NX, NY, 128))
            left.append(jnp.where(tall, copies, 0.0).reshape(NX * NY, 128))
        S[a] = dot_nt(jnp.concatenate(left, axis=1), VT[...]).reshape(NX, NY, NZ)
        return carry

    lax.fori_loop(0, RANK_S, rebuild, 0)

    def spill(c):
        return pltpu.make_async_copy(
            RES.at[:, pl.ds(c * CX, CX)], resid_hbm.at[:, pl.ds(c * CX, CX)], out_sem.at[CHUNKS + c])

    def subtract(x, carry):
        rs = [S[a, x] for a in range(RANK_S)]
        for s in range(SPECIES):
            total = V[2, s, x + 1]
            for a in range(RANK_S):
                total = total - CC[s * RANK_S + a] * rs[a]
            RES[s, x] = total
        return carry

    for c in range(CHUNKS):
        lax.fori_loop(c * CX, (c + 1) * CX, subtract, 0)
        spill(c).start()

    taken(CO.at[pl.ds(0, DY - 1)], sc, rc).wait()
    odd = lax.rem(me, 2)
    result = jnp.zeros((8, 256), F32)
    src_lane = iota((128, 256), 0)
    dst_lane = iota((128, 256), 1)
    b_out, c_out, d_out = dst_lane >> 6, (dst_lane >> 5) & 1, dst_lane & 31
    for d in range(4):
        want = ((c_out + 2 * odd) * 4 + b_out) * 8 + (d_out & 7)
        choose = jnp.logical_and(src_lane == want, (d_out >> 3) == d).astype(F32)
        result = result + dot(CO[d * 8:(d + 1) * 8].reshape(8, 128), choose)
    core_ref[...] = result

    for n in range(4):
        for up in (0, 1):
            @pl.when(has(("x", up)))
            def _():
                copy_x(n, up).wait_send()

            @pl.when(has(("y", up)))
            def _():
                for c in range(CHUNKS):
                    copy_y(n, up, c).wait_send()
    for c in range(CHUNKS):
        save(c).wait()
        spill(c).wait()


def body(v, flow, temp, diff, pre, energy, prod, east, north, vert, comp):
    vmem = pl.BlockSpec(memory_space=pltpu.VMEM)
    smem = pl.BlockSpec(memory_space=pltpu.SMEM)
    anywhere = pl.BlockSpec(memory_space=pl.ANY)
    field = (SPECIES, NX, NY, NZ)
    dma = pltpu.SemaphoreType.DMA
    tiles = lambda n: pltpu.VMEM((n, 8, 128), F32)
    final, resid, core = pl.pallas_call(
        kernel,
        out_shape=(
            jax.ShapeDtypeStruct(field, F32),
            jax.ShapeDtypeStruct(field, F32),
            jax.ShapeDtypeStruct((8, 256), F32),
        ),
        in_specs=[anywhere] * 3 + [smem] * 5 + [vmem] * 3,
        out_specs=(anywhere, anywhere, vmem),
        scratch_shapes=[
            pltpu.VMEM((5, SPECIES, NX + 2, NY, NZ), F32),
            pltpu.VMEM((3, NX, NY, NZ), F32),
            pltpu.VMEM((NX, NY, NZ), F32),
            pltpu.VMEM(field, F32),
            tiles(SPECIES * SPECIES),
            tiles(SPECIES * RANK_S),
            pltpu.VMEM((4, 2, NX, SPECIES, NZ), F32),
            pltpu.VMEM((4, 2, NX, SPECIES, NZ), F32),
            pltpu.VMEM((RANK_S, NX, NY, NZ), F32),
            pltpu.VMEM((NZ, 512), F32),
            tiles(DY),
            pltpu.VMEM((DX, NX, 128), F32),
            tiles(DY),
            tiles(DY),
            tiles(DX),
            tiles(DX),
            tiles(DX),
            tiles(DX),
            tiles(DY),
            tiles(DY),
            pltpu.VMEM((DX, 1, 128), F32),
            pltpu.VMEM((DY, 1, 128), F32),
            pltpu.VMEM(field, F32),
            dma((3,)),
            dma((2 * CHUNKS,)),
            dma((4, 2)), dma((4, 2)), dma((4, 2, CHUNKS)), dma((4, 2, CHUNKS)),
        ] + [dma] * 18,
        compiler_params=pltpu.CompilerParams(
            collective_id=0, has_side_effects=True, vmem_limit_bytes=48 << 20),
        name="flow_tucker",
    )(v, flow, temp, diff, pre, energy, prod, comp, east, north, vert)
    return final, resid, core.reshape(8, 4, 2, 32)


def solution(mesh):
    rows = ("gy", "ga")
    field = P(None, "gx", rows, None)
    in_specs = (
        field, field, P("gx", rows, None), P(), P(), P(), P(),
        P("gx", None), P(rows, None), P(), P(),
    )
    return jax.shard_map(
        body, mesh=mesh, in_specs=in_specs, out_specs=(field, field, field), check_vma=False)
```

time: 861 us -> 119 us (0.14)
  waiting for transfers between devices: 686 us -> 0 us
  Pallas kernels: 0 us -> 112 us
  starting transfers between devices: 82.5 us -> 0 us
  blocking collectives: 39.9 us -> 0 us
  matrix products: 22.9 us -> 0 us
  between operations: 14.9 us -> 0.74 us
    unnamed x4 -> x0, waiting for transfers between devices: 521 us -> none
    pallas_call x0 -> x1, Pallas kernels: none -> 112 us  [body(): pl.pallas_call(kernel, out_shape=(jax.ShapeDtypeStruct(field, F32), jax.S...]
    ppermute x16 -> x0, starting transfers between devices: 82.3 us -> none  [the longest x8 51.3 us: padded_2(): lax.ppermute(lax.slice_in_dim(block, 0, width, axis=dim), axis, backward)]
    all_gather x1 -> x0, waiting for transfers between devices: 64.2 us -> none  [expand(): lax.all_gather(expanded, ('gy', 'ga'), axis=2, tiled=True)]
    reduce_scatter x1 -> x0, waiting for transfers between devices: 63.9 us -> none  [compress(): lax.psum_scatter(partial_value, 'gx', scatter_dimension=1, tiled=True)]
    all_gather x1 -> x0, blocking collectives: 39.9 us -> none  [expand(): lax.all_gather(core_block, 'gx', axis=1, tiled=True)]
    ppermute x16 -> x0, waiting for transfers between devices: 36.8 us -> none  [the longest x8 21.7 us: padded_2(): lax.ppermute(lax.slice_in_dim(block, block.shape[dim] - width, None, axis...]
    dot_general x12 -> x0, matrix products: 22.9 us -> none  [the longest x4 8.12 us: advance_solution(): jnp.einsum('sk,kxyz->sxyz', production_coefficients, reaction_source_term...]
  transfers between devices with their start and end apart: 19 -> 0, of which waited for: 13 -> 0; matrix products, arithmetic and copies ran while one was open for 1% -> 0% of each run, Pallas kernels for 0% -> 0%
where the time goes in v1:
time: 119 us
  Pallas kernels  112 us (94%)
  local copies, waits for them, and re-layouts  6.34 us (5%)
    pallas_call x1, Pallas kernels, body(): pl.pallas_call(kernel, out_shape=(jax.ShapeDtypeStruct(field, F32), jax.S...  112 us
    unnamed x24, local copies, waits for them, and re-layouts  5.64 us

profile of v1, /device:TPU:1, one launch (start us, length us, event | category | flops | bytes accessed | tf_op | source)
XLA Modules:
  0.0 119.1 jit_solution(9875606466717368325)
XLA Ops:
  0.6 0.0 copy-start.9
  0.6 0.0 copy-start.2
  0.7 0.0 copy-start.4
  0.7 0.0 copy-start.6
  0.7 0.0 copy-start.7
  0.7 0.0 copy-start.8
  0.7 0.9 copy.15.vert_ref
  1.6 0.0 copy-done.9
  1.6 0.0 copy-start.3
  1.6 0.0 copy-start.5
  1.6 0.1 copy.14.comp_ref
  1.7 0.0 copy-done.2
  1.7 0.0 copy-done.4
  1.7 0.0 copy-done.6
  1.7 0.0 copy-done.7
  1.7 0.0 copy-done.8
  1.7 0.6 copy-done.3
  2.3 0.0 copy-done.5
  2.3 0.0 copy-start
  2.3 1.2 %copy-done = f32[16,16,8,128]{3,2,1,0:T(8,128)S(1)} copy-done((f32[16,16,8,128]{3,2,1,0:T(8,128)S(1)}, f32[16,16,8,128]{3,2,1,0:T(8,128)}, u32[]{:S(2)}) %copy-start) | copy-done | bytes 1048600
  3.5 0.0 copy-start.1
  3.5 0.9 copy-done.1
  4.4 112.0 %flow_tucker.1 = (f32[16,16,8,128]{3,2,1,0:T(8,128)S(1)}, f32[16,16,8,128]{3,2,1,0:T(8,128)S(1)}, f32[8,256]{1,0:T(8,128)S(1)}) custom-call(f32[16,16,8,128]{3,2,1,0:T(8,128)S(1)} %copy-done, f32[3,16,8,128]{3,2,1,0:T(8,128)S(1)} %copy-done.1, f32[16,8,128]{2,1,0:T(8,128)S(1)} %copy-done.2, f32[16]{0:T(128)S(1)} %copy-done.6, f32[16]{0:T(128)S(1)} %copy-done.7, ...), custom_call_target="tpu_custom_call" | custom-call | tf_op jit(solution)/shard_map/flow_tucker/pallas_call | solution.py:476
  116.5 0.7 reshape.9
  117.2 1.0 copy.18
  118.1 1.0 copy.19
Async XLA Ops:
  0.6 0.9 copy-start.9
  0.6 1.0 copy-start.2
  0.7 1.0 copy-start.4
  0.7 1.0 copy-start.6
  0.7 1.0 copy-start.7
  0.7 1.0 copy-start.8
  1.6 0.7 copy-start.3
  1.6 0.7 copy-start.5
  2.3 1.2 %copy-start = (f32[16,16,8,128]{3,2,1,0:T(8,128)S(1)}, f32[16,16,8,128]{3,2,1,0:T(8,128)}, u32[]{:S(2)}) copy-start(f32[16,16,8,128]{3,2,1,0:T(8,128)} %v_hbm.1) | copy-start | bytes 3145732
  3.5 0.9 copy-start.1

commit v2 on v1

--- a/solution.py
+++ b/solution.py
@@ -22,6 +22,7 @@
 CHUNKS = 4
 CX = NX // CHUNKS
 ORDER = (0, 3, 1, 2)
+EARLY, LATE = ORDER[:CHUNKS // 2], ORDER[CHUNKS // 2:]
 
 
 def dot(a, b):
@@ -42,10 +43,10 @@
 
 def kernel(
     v_hbm, flow_hbm, temp_hbm, diff_ref, pre_ref, energy_ref, prod_ref, comp_ref,
-    east_ref, north_ref, vert_ref,
-    final_hbm, resid_hbm, core_ref,
+    east_hbm, north_hbm, vert_hbm,
+    final_ref, snap_ref, rec_ref, core_ref,
     V, F, T, K, PC, CC, HY, FY, S, VT, NF, EF,
-    PB, G, QB, H, MB, Q8, UB, W, CS, CO, RES,
+    PB, G, QB, H, MB, Q8, UB, W, CS, CO, east_ref, north_ref, vert_ref,
     load_sem, out_sem,
     sx, rx, sy, ry,
     sn1, rn1, sn2, rn2, se1, re1, se2, re2,
@@ -80,9 +81,14 @@
     load_v = pltpu.make_async_copy(v_hbm, V.at[0, :, pl.ds(1, NX)], load_sem.at[0])
     load_f = pltpu.make_async_copy(flow_hbm, F, load_sem.at[1])
     load_t = pltpu.make_async_copy(temp_hbm, T, load_sem.at[2])
+    small = [
+        pltpu.make_async_copy(east_hbm, east_ref, load_sem.at[3]),
+        pltpu.make_async_copy(north_hbm, north_ref, load_sem.at[4]),
+        pltpu.make_async_copy(vert_hbm, vert_ref, load_sem.at[5]),
+    ]
     load_v.start()
-    load_f.start()
-    load_t.start()
+    for load in [load_f, load_t] + small:
+        load.start()
 
     zeros = jnp.zeros((SPECIES, NY, NZ), F32)
     zface = jnp.zeros((NX, SPECIES, NZ), F32)
@@ -169,6 +175,8 @@
     for c in ORDER:
         send_y(0, c)
 
+    for load in small:
+        load.wait()
     old = iota((64, 128), 0)
     spread = (iota((64, 128), 1) == (old >> 2) * 8 + (old & 3)).astype(F32)
     NF[me] = dot(north_ref[...], spread)
@@ -223,14 +231,14 @@
         for k in range(SPECIES):
             PC[s * SPECIES + k] = jnp.full((8, 128), prod_ref[s, k], F32)
         for a in range(RANK_S):
-            CC[s * RANK_S + a] = jnp.full((8, 128), comp_ref[s, a], F32)
+            CC[s * RANK_S + a] = jnp.full((8, 128), comp_ref[a, s], F32)
         return c
 
     lax.fori_loop(0, SPECIES, splat, 0)
 
     spot = iota((32, 512), 1)
     pick = (iota((32, 512), 0) == (spot >> 7) * 8 + (spot & 7)).astype(F32)
-    VT[...] = dot(vert_ref[...], pick)
+    VT[...] = dot_tn(vert_ref[...], pick)
 
     row = iota((NY, NZ), 0)
     lane = iota((NY, NZ), 1)
@@ -260,7 +268,7 @@
                 FY[n + 1, 0, x, s:s + 1, :] = total[0:1, :]
                 FY[n + 1, 1, x, s:s + 1, :] = total[NY - 1:NY, :]
 
-    def step(n, c):
+    def step(n, c, send=True):
         last = n == 3
         recv_y(n, c)
         if c == 0:
@@ -274,7 +282,8 @@
 
         lax.fori_loop(0, CX, body, 0)
         if not last:
-            send_y(n + 1, c)
+            if send:
+                send_y(n + 1, c)
             if c == 0:
                 send_x(n + 1, 0)
             if c == CHUNKS - 1:
@@ -285,7 +294,7 @@
     def save(c):
         return pltpu.make_async_copy(
             V.at[4, :, pl.ds(1 + c * CX, CX)],
-            final_hbm.at[:, pl.ds(c * CX, CX)],
+            final_ref.at[:, pl.ds(c * CX, CX)],
             out_sem.at[c])
 
     step(0, ORDER[0])
@@ -297,9 +306,6 @@
         e2(k).start()
     for c in ORDER[1:]:
         step(0, c)
-    for c in ORDER:
-        step(1, c)
-
     def squash(x, carry):
         vs = [V[2, s, x + 1] for s in range(SPECIES)]
         for a in range(RANK_S):
@@ -309,33 +315,46 @@
             S[a, x] = total
         return carry
 
-    lax.fori_loop(0, NX, squash, 0)
-    wide = ((iota((NX, NY, 512), 2) & 127) >> 3) == iota((NX, NY, 512), 0)
-
-    def project(a, carry):
-        out = dot(S[a].reshape(NX * NY, NZ), VT[...]).reshape(NX, NY, 512)
-        out = jnp.sum(jnp.where(wide, out, 0.0), axis=0)
-        for d in range(4):
-            PB[a * 4 + d] = out[:, d * 128:(d + 1) * 128]
-        return carry
-
-    lax.fori_loop(0, RANK_S, project, 0)
+    def project(c):
+        where = ((iota((CX, NY, 512), 2) & 127) >> 3) == iota((CX, NY, 512), 0) + c * CX
+        part = pl.ds(c * CX, CX)
+
+        def one(a, carry):
+            out = dot(S[a, part].reshape(CX * NY, NZ), VT[...]).reshape(CX, NY, 512)
+            out = jnp.sum(jnp.where(where, out, 0.0), axis=0)
+            for d in range(4):
+                tile = out[:, d * 128:(d + 1) * 128]
+                PB[a * 4 + d] = tile if c == ORDER[0] else PB[a * 4 + d] + tile
+            return carry
+
+        lax.fori_loop(0, RANK_S, one, 0)
+
+    for c in ORDER:
+        step(1, c, send=c in EARLY)
+        lax.fori_loop(c * CX, (c + 1) * CX, squash, 0)
+        project(c)
+
+    def each_y(start):
+        for g in (2, 1, 3, 0):
+            def go(o, carry, g=g):
+                start(lax.rem(gy + o, GY) * GA + lax.rem(ga + g, GA))
+                return carry
+            lax.fori_loop(0 if g else 1, GY, go, 0)
 
     def to_y(src, dst, send, recv):
-        def go(k, carry):
-            j = lax.rem(me + k, DY)
+        def start(j):
             pltpu.make_async_remote_copy(
                 src.at[j], dst.at[me], send, recv, device_id=at_y(j), device_id_type=MESH).start()
-            return carry
-        lax.fori_loop(1, DY, go, 0)
+        each_y(start)
 
     def to_x(src, dst, send, recv):
-        def go(k, carry):
-            m = lax.rem(gx + k, DX)
-            pltpu.make_async_remote_copy(
-                src.at[m], dst.at[gx], send, recv, device_id=at_x(m), device_id_type=MESH).start()
-            return carry
-        lax.fori_loop(1, DX, go, 0)
+        for g in (2, 1, 3, 0):
+            def go(o, carry, g=g):
+                m = lax.rem(xh + g, DX // ZL) * ZL + lax.rem(zl + o, ZL)
+                pltpu.make_async_remote_copy(
+                    src.at[m], dst.at[gx], send, recv, device_id=at_x(m), device_id_type=MESH).start()
+                return carry
+            lax.fori_loop(0 if g else 1, ZL, go, 0)
 
     def done_y(ref, send, recv):
         taken(ref.at[pl.ds(0, DY - 1)], send, recv).wait()
@@ -345,9 +364,12 @@
 
     to_y(PB, G, sp, rp)
     G[me] = PB[me]
-
-    for c in ORDER:
-        step(2, c)
+    keep = pltpu.make_async_copy(V.at[2, :, pl.ds(1, NX)], snap_ref, out_sem.at[CHUNKS])
+    keep.start()
+    for c in LATE:
+        send_y(2, c)
+    for c in EARLY:
+        step(2, c, send=False)
 
     taken(NF.at[pl.ds(0, GA * (GY - 1))], sn2, rn2).wait()
     taken(EF.at[pl.ds(0, ZL * (DX // ZL - 1))], se2, re2).wait()
@@ -356,8 +378,10 @@
     QB[...] = dot_tn(north, G[...].reshape(DY * NY, 128)).reshape(DX, 8, 128)
     to_x(QB, H, sq, rq)
     H[gx] = QB[gx]
-
-    step(3, ORDER[0])
+    for c in EARLY:
+        send_y(3, c)
+    for c in LATE:
+        step(2, c, send=False)
 
     done_x(H, sq, rq)
     own_x = (iota((DX, NX, 128), 2) >> 3) == iota((DX, NX, 128), 1)
@@ -386,8 +410,9 @@
         MB[:, c, :] = jnp.zeros((DX, 128), F32)
     to_x(MB, Q8, sm, rm)
     Q8[gx] = MB[gx]
-
-    step(3, ORDER[1])
+    for c in LATE:
+        send_y(3, c)
+    step(3, ORDER[0])
 
     done_x(Q8, sm, rm)
     UB[...] = dot(NF[...].reshape(DY * NY, 128), Q8[...].reshape(DX * 8, 128)).reshape(DY, NY, 128)
@@ -397,17 +422,15 @@
         CS[m] = Q8[m, 4:5, :]
     own = CO.at[lax.rem(me, 4) * 8 + me // 4]
 
-    def core_go(k, carry):
-        j = lax.rem(me + k, DY)
+    def core_go(j):
         pltpu.make_async_remote_copy(
             CS.at[j // 2], own, sc, rc, device_id=at_y(j), device_id_type=MESH).start()
-        return carry
-
-    lax.fori_loop(1, DY, core_go, 0)
+
+    each_y(core_go)
     CO[lax.rem(me, 4) * 8 + me // 4] = CS[me // 2]
 
-    step(3, ORDER[2])
-    step(3, ORDER[3])
+    for c in ORDER[1:]:
+        step(3, c)
 
     done_y(W, su, ru)
     tall = (iota((NX, NY, 128), 2) >> 3) == iota((NX, NY, 128), 0)
@@ -417,27 +440,10 @@
         for d in range(4):
             copies = jnp.broadcast_to(W[a * 4 + d][None], (NX, NY, 128))
             left.append(jnp.where(tall, copies, 0.0).reshape(NX * NY, 128))
-        S[a] = dot_nt(jnp.concatenate(left, axis=1), VT[...]).reshape(NX, NY, NZ)
+        rec_ref[a] = dot_nt(jnp.concatenate(left, axis=1), VT[...]).reshape(NX, NY, NZ)
         return carry
 
     lax.fori_loop(0, RANK_S, rebuild, 0)
-
-    def spill(c):
-        return pltpu.make_async_copy(
-            RES.at[:, pl.ds(c * CX, CX)], resid_hbm.at[:, pl.ds(c * CX, CX)], out_sem.at[CHUNKS + c])
-
-    def subtract(x, carry):
-        rs = [S[a, x] for a in range(RANK_S)]
-        for s in range(SPECIES):
-            total = V[2, s, x + 1]
-            for a in range(RANK_S):
-                total = total - CC[s * RANK_S + a] * rs[a]
-            RES[s, x] = total
-        return carry
-
-    for c in range(CHUNKS):
-        lax.fori_loop(c * CX, (c + 1) * CX, subtract, 0)
-        spill(c).start()
 
     taken(CO.at[pl.ds(0, DY - 1)], sc, rc).wait()
     odd = lax.rem(me, 2)
@@ -449,7 +455,8 @@
         want = ((c_out + 2 * odd) * 4 + b_out) * 8 + (d_out & 7)
         choose = jnp.logical_and(src_lane == want, (d_out >> 3) == d).astype(F32)
         result = result + dot(CO[d * 8:(d + 1) * 8].reshape(8, 128), choose)
-    core_ref[...] = result
+    for i in range(8):
+        core_ref[i] = result[:, i * 32:(i + 1) * 32]
 
     for n in range(4):
         for up in (0, 1):
@@ -463,25 +470,55 @@
                     copy_y(n, up, c).wait_send()
     for c in range(CHUNKS):
         save(c).wait()
+    keep.wait()
+
+
+def finish(final_ref, snap_ref, rec_ref, comp_ref, final_hbm, resid_hbm, RES, sem):
+    out = pltpu.make_async_copy(final_ref, final_hbm, sem.at[CHUNKS])
+    out.start()
+
+    def spill(c):
+        return pltpu.make_async_copy(
+            RES.at[:, pl.ds(c * CX, CX)], resid_hbm.at[:, pl.ds(c * CX, CX)], sem.at[c])
+
+    def subtract(x, carry):
+        rs = [rec_ref[a, x] for a in range(RANK_S)]
+        for s in range(SPECIES):
+            total = snap_ref[s, x]
+            for a in range(RANK_S):
+                total = total - comp_ref[a, s] * rs[a]
+            RES[s, x] = total
+        return carry
+
+    for c in range(CHUNKS):
+        lax.fori_loop(c * CX, (c + 1) * CX, subtract, 0)
+        spill(c).start()
+    for c in range(CHUNKS):
         spill(c).wait()
+    out.wait()
 
 
 def body(v, flow, temp, diff, pre, energy, prod, east, north, vert, comp):
     vmem = pl.BlockSpec(memory_space=pltpu.VMEM)
+    hbm = pl.BlockSpec(memory_space=pltpu.HBM)
     smem = pl.BlockSpec(memory_space=pltpu.SMEM)
-    anywhere = pl.BlockSpec(memory_space=pl.ANY)
     field = (SPECIES, NX, NY, NZ)
     dma = pltpu.SemaphoreType.DMA
     tiles = lambda n: pltpu.VMEM((n, 8, 128), F32)
-    final, resid, core = pl.pallas_call(
+    comp_t = comp.T
+    v, flow, temp, east, north, vert, diff, pre, energy, prod, comp = [
+        pltpu.with_memory_space_constraint(a, pltpu.HBM)
+        for a in (v, flow, temp, east, north, vert.T, diff, pre, energy, prod, comp_t)]
+    final, snap, rec, core = pl.pallas_call(
         kernel,
         out_shape=(
             jax.ShapeDtypeStruct(field, F32),
             jax.ShapeDtypeStruct(field, F32),
-            jax.ShapeDtypeStruct((8, 256), F32),
+            jax.ShapeDtypeStruct((RANK_S, NX, NY, NZ), F32),
+            jax.ShapeDtypeStruct((8, 8, 32), F32),
         ),
-        in_specs=[anywhere] * 3 + [smem] * 5 + [vmem] * 3,
-        out_specs=(anywhere, anywhere, vmem),
+        in_specs=[hbm] * 3 + [smem] * 5 + [hbm] * 3,
+        out_specs=(vmem,) * 4,
         scratch_shapes=[
             pltpu.VMEM((5, SPECIES, NX + 2, NY, NZ), F32),
             pltpu.VMEM((3, NX, NY, NZ), F32),
@@ -505,8 +542,8 @@
             tiles(DY),
             pltpu.VMEM((DX, 1, 128), F32),
             pltpu.VMEM((DY, 1, 128), F32),
-            pltpu.VMEM(field, F32),
-            dma((3,)),
+            pltpu.VMEM((NX, 64), F32), pltpu.VMEM((NY, 64), F32), pltpu.VMEM((32, NZ), F32),
+            dma((6,)),
             dma((2 * CHUNKS,)),
             dma((4, 2)), dma((4, 2)), dma((4, 2, CHUNKS)), dma((4, 2, CHUNKS)),
         ] + [dma] * 18,
@@ -514,7 +551,16 @@
             collective_id=0, has_side_effects=True, vmem_limit_bytes=48 << 20),
         name="flow_tucker",
     )(v, flow, temp, diff, pre, energy, prod, comp, east, north, vert)
-    return final, resid, core.reshape(8, 4, 2, 32)
+    final, resid = pl.pallas_call(
+        finish,
+        out_shape=(jax.ShapeDtypeStruct(field, F32),) * 2,
+        in_specs=[vmem] * 3 + [smem],
+        out_specs=(hbm, hbm),
+        scratch_shapes=[pltpu.VMEM(field, F32), dma((CHUNKS + 1,))],
+        compiler_params=pltpu.CompilerParams(vmem_limit_bytes=16 << 20),
+        name="finish",
+    )(final, snap, rec, comp)
+    return final, resid, core.transpose(1, 0, 2).reshape(8, 4, 2, 32)
 
 
 def solution(mesh):

time: 119 us -> 110 us (0.924)
  local copies, waits for them, and re-layouts: 6.34 us -> 0.63 us
  Pallas kernels: 112 us -> 108 us
    pallas_call x1, Pallas kernels: 112 us -> 105 us  [body(): pl.pallas_call(kernel, out_shape=(jax.ShapeDtypeStruct(field, F32), jax.S...]
    unnamed x24 -> x1, local copies, waits for them, and re-layouts: 5.64 us -> 0.63 us
    pallas_call x0 -> x1, Pallas kernels: none -> 2.43 us  [body(): pl.pallas_call(finish, out_shape=(jax.ShapeDtypeStruct(field, F32),) * 2,...]
where the time goes in v2:
time: 110 us; the launch traced here: 109 us
  Pallas kernels  108 us (98%)
    pallas_call x1, Pallas kernels, body(): pl.pallas_call(kernel, out_shape=(jax.ShapeDtypeStruct(field, F32), jax.S...  105 us
    pallas_call x1, Pallas kernels, body(): pl.pallas_call(finish, out_shape=(jax.ShapeDtypeStruct(field, F32),) * 2,...  2.43 us

profile of v2, /device:TPU:1, one launch (start us, length us, event | category | flops | bytes accessed | tf_op | source)
XLA Modules:
  0.0 109.0 jit_solution(4638304778590750535)
XLA Ops:
  0.6 105.3 %flow_tucker.1 = (f32[16,16,8,128]{3,2,1,0:T(8,128)S(1)}, f32[16,16,8,128]{3,2,1,0:T(8,128)S(1)}, f32[8,16,8,128]{3,2,1,0:T(8,128)S(1)}, f32[8,8,32]{2,1,0:T(8,128)S(1)}) custom-call(f32[16,16,8,128]{3,2,1,0:T(8,128)} %v_hbm.1, f32[3,16,8,128]{3,2,1,0:T(8,128)} %flow_hbm.1, f32[16,8,128]{2,1,0:T(8,128)} %temp_hbm.1, f32[16]{0:T(128)} %diff_ref.1, ...), custom_call_target="tpu_custom_call" | custom-call | tf_op jit(solution)/shard_map/flow_tucker/pallas_call | solution.py:512
  105.9 2.4 %finish.1 = (f32[16,16,8,128]{3,2,1,0:T(8,128)}, f32[16,16,8,128]{3,2,1,0:T(8,128)}) custom-call(f32[16,16,8,128]{3,2,1,0:T(8,128)S(1)} %get-tuple-element.9.final_ref, f32[16,16,8,128]{3,2,1,0:T(8,128)S(1)} %get-tuple-element.10.snap_ref, f32[8,16,8,128]{3,2,1,0:T(8,128)S(1)} %get-tuple-element.11.rec_ref, f32[8,16]{1,0:T(8,128)} %bitcast.8), custom_call_target="tpu_custom_call" | custom-call | tf_op jit(solution)/shard_map/finish/pallas_call | solution.py:554
  108.4 0.6 copy.14

commit v3 on v2

--- a/solution.py
+++ b/solution.py
@@ -46,7 +46,7 @@
     east_hbm, north_hbm, vert_hbm,
     final_ref, snap_ref, rec_ref, core_ref,
     V, F, T, K, PC, CC, HY, FY, S, VT, NF, EF,
-    PB, G, QB, H, MB, Q8, UB, W, CS, CO, east_ref, north_ref, vert_ref,
+    PB, G, QB, H, MB, Q8, UB, W, CS, CO, QS, east_ref, north_ref, vert_ref,
     load_sem, out_sem,
     sx, rx, sy, ry,
     sn1, rn1, sn2, rn2, se1, re1, se2, re2,
@@ -177,10 +177,8 @@
 
     for load in small:
         load.wait()
-    old = iota((64, 128), 0)
-    spread = (iota((64, 128), 1) == (old >> 2) * 8 + (old & 3)).astype(F32)
-    NF[me] = dot(north_ref[...], spread)
     eye = (iota((64, 128), 1) == iota((64, 128), 0)).astype(F32)
+    NF[me] = dot(north_ref[...], eye)
     EF[gx] = dot(east_ref[...], eye)
 
     def n1(k):
@@ -236,8 +234,8 @@
 
     lax.fori_loop(0, SPECIES, splat, 0)
 
-    spot = iota((32, 512), 1)
-    pick = (iota((32, 512), 0) == (spot >> 7) * 8 + (spot & 7)).astype(F32)
+    spot = iota((32, 256), 1)
+    pick = (iota((32, 256), 0) == (spot >> 7) * 16 + (spot & 15)).astype(F32)
     VT[...] = dot_tn(vert_ref[...], pick)
 
     row = iota((NY, NZ), 0)
@@ -316,15 +314,14 @@
         return carry
 
     def project(c):
-        where = ((iota((CX, NY, 512), 2) & 127) >> 3) == iota((CX, NY, 512), 0) + c * CX
+        where = ((iota((CX, NY, 256), 2) & 127) >> 4) == iota((CX, NY, 256), 1)
         part = pl.ds(c * CX, CX)
 
         def one(a, carry):
-            out = dot(S[a, part].reshape(CX * NY, NZ), VT[...]).reshape(CX, NY, 512)
-            out = jnp.sum(jnp.where(where, out, 0.0), axis=0)
-            for d in range(4):
-                tile = out[:, d * 128:(d + 1) * 128]
-                PB[a * 4 + d] = tile if c == ORDER[0] else PB[a * 4 + d] + tile
+            out = dot(S[a, part].reshape(CX * NY, NZ), VT[...]).reshape(CX, NY, 256)
+            out = jnp.sum(jnp.where(where, out, 0.0), axis=1)
+            for d in range(2):
+                PB[a * 2 + d, c * CX:(c + 1) * CX, :] = out[:, d * 128:(d + 1) * 128]
             return carry
 
         lax.fori_loop(0, RANK_S, one, 0)
@@ -347,23 +344,27 @@
                 src.at[j], dst.at[me], send, recv, device_id=at_y(j), device_id_type=MESH).start()
         each_y(start)
 
-    def to_x(src, dst, send, recv):
+    def each_x(start):
         for g in (2, 1, 3, 0):
             def go(o, carry, g=g):
-                m = lax.rem(xh + g, DX // ZL) * ZL + lax.rem(zl + o, ZL)
-                pltpu.make_async_remote_copy(
-                    src.at[m], dst.at[gx], send, recv, device_id=at_x(m), device_id_type=MESH).start()
+                start(lax.rem(xh + g, DX // ZL) * ZL + lax.rem(zl + o, ZL))
                 return carry
             lax.fori_loop(0 if g else 1, ZL, go, 0)
 
+    def to_x(src, dst, send, recv):
+        def start(m):
+            pltpu.make_async_remote_copy(
+                src.at[m], dst.at[gx], send, recv, device_id=at_x(m), device_id_type=MESH).start()
+        each_x(start)
+
     def done_y(ref, send, recv):
         taken(ref.at[pl.ds(0, DY - 1)], send, recv).wait()
 
     def done_x(ref, send, recv):
         taken(ref.at[pl.ds(0, DX - 1)], send, recv).wait()
 
-    to_y(PB, G, sp, rp)
-    G[me] = PB[me]
+    to_x(PB, G, sp, rp)
+    G[gx] = PB[gx]
     keep = pltpu.make_async_copy(V.at[2, :, pl.ds(1, NX)], snap_ref, out_sem.at[CHUNKS])
     keep.start()
     for c in LATE:
@@ -373,88 +374,96 @@
 
     taken(NF.at[pl.ds(0, GA * (GY - 1))], sn2, rn2).wait()
     taken(EF.at[pl.ds(0, ZL * (DX // ZL - 1))], se2, re2).wait()
-    done_y(G, sp, rp)
-    north = NF[...].reshape(DY * NY, 128)
-    QB[...] = dot_tn(north, G[...].reshape(DY * NY, 128)).reshape(DX, 8, 128)
-    to_x(QB, H, sq, rq)
-    H[gx] = QB[gx]
+    done_x(G, sp, rp)
+    east = EF[...].reshape(DX * NX, 128)
+    pairs = dot_tn(east, G[...].reshape(DX * NX, 128))
+    for j in range(DY):
+        QB[j] = pairs[2 * j:2 * j + 2, :]
+    to_y(QB, H, sq, rq)
+    H[me] = QB[me]
     for c in EARLY:
         send_y(3, c)
     for c in LATE:
         step(2, c, send=False)
 
-    done_x(H, sq, rq)
-    own_x = (iota((DX, NX, 128), 2) >> 3) == iota((DX, NX, 128), 1)
+    done_y(H, sq, rq)
+    own_y = (iota((DY, NY, 128), 2) >> 4) == iota((DY, NY, 128), 1)
     blocks = []
-    for c in range(4):
-        spread_h = jnp.broadcast_to(H[:, c:c + 1, :], (DX, NX, 128))
-        blocks.append(jnp.where(own_x, spread_h, 0.0).reshape(DX * NX, 128))
-    east = EF[...].reshape(DX * NX, 128)
-    core = dot_tn(east, jnp.concatenate(blocks, axis=1))
+    for b in range(2):
+        spread_h = jnp.broadcast_to(H[:, b:b + 1, :], (DY, NY, 128))
+        blocks.append(jnp.where(own_y, spread_h, 0.0).reshape(DY * NY, 128))
+    north = NF[...].reshape(DY * NY, 128)
+    core = dot_tn(north, jnp.concatenate(blocks, axis=1))
     piece = jnp.zeros((128, 128), F32)
-    slot = iota((128, 128), 1) >> 3
-    b_low = iota((128, 128), 0) & 3
+    slot = iota((128, 128), 1) >> 4
+    c_low = iota((128, 128), 0) & 1
     parts = []
-    for c in range(4):
-        part = core[:, c * 128:(c + 1) * 128]
-        for shift in (64, 32, 16, 8):
+    for b in range(2):
+        part = core[:, b * 128:(b + 1) * 128]
+        for shift in (64, 32, 16):
             part = part + pltpu.roll(part, shift, 1)
         parts.append(part)
-        piece = piece + jnp.where(slot == c * 4 + b_low, part, 0.0)
-    out = dot(east, jnp.concatenate(parts, axis=1))
-    for c in range(4):
-        block = out[:, c * 128:(c + 1) * 128].reshape(DX, NX, 128)
-        MB[:, c, :] = jnp.sum(jnp.where(own_x, block, 0.0), axis=1)
-    MB[:, 4, :] = jnp.sum(piece[:64].reshape(DX, 4, 128), axis=1)
-    for c in range(5, 8):
-        MB[:, c, :] = jnp.zeros((DX, 128), F32)
-    to_x(MB, Q8, sm, rm)
-    Q8[gx] = MB[gx]
+        piece = piece + jnp.where(slot == b * 2 + c_low, part, 0.0)
+    out = dot(north, jnp.concatenate(parts, axis=1))
+    for b in range(2):
+        block = out[:, b * 128:(b + 1) * 128].reshape(DY, NY, 128)
+        MB[:, b, :] = jnp.sum(jnp.where(own_y, block, 0.0), axis=1)
+    MB[:, 2, :] = jnp.sum(piece[:64].reshape(DY, 2, 128), axis=1)
+    MB[:, 3, :] = jnp.zeros((DY, 128), F32)
+    to_y(MB, Q8, sm, rm)
+    Q8[me] = MB[me]
     for c in LATE:
         send_y(3, c)
     step(3, ORDER[0])
 
-    done_x(Q8, sm, rm)
-    UB[...] = dot(NF[...].reshape(DY * NY, 128), Q8[...].reshape(DX * 8, 128)).reshape(DY, NY, 128)
-    to_y(UB, W, su, ru)
-    W[me] = UB[me]
-    for m in range(DX):
-        CS[m] = Q8[m, 4:5, :]
-    own = CO.at[lax.rem(me, 4) * 8 + me // 4]
-
-    def core_go(j):
+    QS[64:, :] = jnp.zeros((64, 128), F32)
+    done_y(Q8, sm, rm)
+    for j in range(DY):
+        QS[2 * j:2 * j + 2, :] = Q8[j, 0:2, :]
+    UB[...] = dot(EF[...].reshape(DX * NX, 128), QS[...]).reshape(DX, NX, 128)
+    to_x(UB, W, su, ru)
+    W[gx] = UB[gx]
+    for j in range(DY):
+        CS[j // 2, j % 2] = Q8[j, 2:3, :]
+    home = lax.rem(gx, 2) * 8 + gx // 2
+
+    def core_go(m):
         pltpu.make_async_remote_copy(
-            CS.at[j // 2], own, sc, rc, device_id=at_y(j), device_id_type=MESH).start()
-
-    each_y(core_go)
-    CO[lax.rem(me, 4) * 8 + me // 4] = CS[me // 2]
+            CS.at[m], CO.at[home], sc, rc, device_id=at_x(m), device_id_type=MESH).start()
+
+    each_x(core_go)
+    CO[home] = CS[gx]
 
     for c in ORDER[1:]:
         step(3, c)
 
-    done_y(W, su, ru)
-    tall = (iota((NX, NY, 128), 2) >> 3) == iota((NX, NY, 128), 0)
+    done_x(W, su, ru)
+    own_row = (iota((NY, 128), 1) >> 4) == iota((NY, 128), 0)
 
     def rebuild(a, carry):
         left = []
-        for d in range(4):
-            copies = jnp.broadcast_to(W[a * 4 + d][None], (NX, NY, 128))
-            left.append(jnp.where(tall, copies, 0.0).reshape(NX * NY, 128))
+        for d in range(2):
+            rows = []
+            for x in range(NX):
+                copies = jnp.broadcast_to(W[a * 2 + d, x:x + 1, :], (NY, 128))
+                rows.append(jnp.where(own_row, copies, 0.0))
+            left.append(jnp.concatenate(rows, axis=0))
         rec_ref[a] = dot_nt(jnp.concatenate(left, axis=1), VT[...]).reshape(NX, NY, NZ)
         return carry
 
     lax.fori_loop(0, RANK_S, rebuild, 0)
 
-    taken(CO.at[pl.ds(0, DY - 1)], sc, rc).wait()
-    odd = lax.rem(me, 2)
+    taken(CO.at[pl.ds(0, DX - 1)], sc, rc).wait()
     result = jnp.zeros((8, 256), F32)
     src_lane = iota((128, 256), 0)
     dst_lane = iota((128, 256), 1)
     b_out, c_out, d_out = dst_lane >> 6, (dst_lane >> 5) & 1, dst_lane & 31
-    for d in range(4):
-        want = ((c_out + 2 * odd) * 4 + b_out) * 8 + (d_out & 7)
-        choose = jnp.logical_and(src_lane == want, (d_out >> 3) == d).astype(F32)
-        result = result + dot(CO[d * 8:(d + 1) * 8].reshape(8, 128), choose)
+    want = ((b_out & 1) * 2 + c_out) * 16 + (d_out & 15)
+    for d in range(2):
+        for b in range(2):
+            here = jnp.logical_and((b_out >> 1) == b, (d_out >> 4) == d)
+            choose = jnp.logical_and(src_lane == want, here).astype(F32)
+            result = result + dot(CO[d * 8:(d + 1) * 8, b].reshape(8, 128), choose)
     for i in range(8):
         core_ref[i] = result[:, i * 32:(i + 1) * 32]
 
@@ -529,19 +538,20 @@
             pltpu.VMEM((4, 2, NX, SPECIES, NZ), F32),
             pltpu.VMEM((4, 2, NX, SPECIES, NZ), F32),
             pltpu.VMEM((RANK_S, NX, NY, NZ), F32),
-            pltpu.VMEM((NZ, 512), F32),
+            pltpu.VMEM((NZ, 256), F32),
             tiles(DY),
             pltpu.VMEM((DX, NX, 128), F32),
-            tiles(DY),
-            tiles(DY),
-            tiles(DX),
-            tiles(DX),
-            tiles(DX),
-            tiles(DX),
-            tiles(DY),
-            tiles(DY),
-            pltpu.VMEM((DX, 1, 128), F32),
-            pltpu.VMEM((DY, 1, 128), F32),
+            pltpu.VMEM((DX, NX, 128), F32),
+            pltpu.VMEM((DX, NX, 128), F32),
+            pltpu.VMEM((DY, 2, 128), F32),
+            pltpu.VMEM((DY, 2, 128), F32),
+            pltpu.VMEM((DY, 4, 128), F32),
+            pltpu.VMEM((DY, 4, 128), F32),
+            pltpu.VMEM((DX, NX, 128), F32),
+            pltpu.VMEM((DX, NX, 128), F32),
+            pltpu.VMEM((DX, 2, 1, 128), F32),
+            pltpu.VMEM((DX, 2, 1, 128), F32),
+            pltpu.VMEM((128, 128), F32),
             pltpu.VMEM((NX, 64), F32), pltpu.VMEM((NY, 64), F32), pltpu.VMEM((32, NZ), F32),
             dma((6,)),
             dma((2 * CHUNKS,)),

time: 110 us -> 106 us (0.964)
  Pallas kernels: 108 us -> 105 us
    pallas_call x1, Pallas kernels: 105 us -> 102 us  [body(): pl.pallas_call(kernel, out_shape=(jax.ShapeDtypeStruct(field, F32), jax.S...]
where the time goes in v3:
time: 106 us
  Pallas kernels  105 us (99%)
    pallas_call x1, Pallas kernels, body(): pl.pallas_call(kernel, out_shape=(jax.ShapeDtypeStruct(field, F32), jax.S...  102 us
    pallas_call x1, Pallas kernels, body(): pl.pallas_call(finish, out_shape=(jax.ShapeDtypeStruct(field, F32),) * 2,...  2.43 us

profile of v3, /device:TPU:1, one launch (start us, length us, event | category | flops | bytes accessed | tf_op | source)
XLA Modules:
  0.0 105.9 jit_solution(13442823924508125100)
XLA Ops:
  0.6 102.2 %flow_tucker.1 = (f32[16,16,8,128]{3,2,1,0:T(8,128)S(1)}, f32[16,16,8,128]{3,2,1,0:T(8,128)S(1)}, f32[8,16,8,128]{3,2,1,0:T(8,128)S(1)}, f32[8,8,32]{2,1,0:T(8,128)S(1)}) custom-call(f32[16,16,8,128]{3,2,1,0:T(8,128)} %v_hbm.1, f32[3,16,8,128]{3,2,1,0:T(8,128)} %flow_hbm.1, f32[16,8,128]{2,1,0:T(8,128)} %temp_hbm.1, f32[16]{0:T(128)} %diff_ref.1, ...), custom_call_target="tpu_custom_call" | custom-call | tf_op jit(solution)/shard_map/flow_tucker/pallas_call | solution.py:521
  102.9 2.4 %finish.1 = (f32[16,16,8,128]{3,2,1,0:T(8,128)}, f32[16,16,8,128]{3,2,1,0:T(8,128)}) custom-call(f32[16,16,8,128]{3,2,1,0:T(8,128)S(1)} %get-tuple-element.9.final_ref, f32[16,16,8,128]{3,2,1,0:T(8,128)S(1)} %get-tuple-element.10.snap_ref, f32[8,16,8,128]{3,2,1,0:T(8,128)S(1)} %get-tuple-element.11.rec_ref, f32[8,16]{1,0:T(8,128)} %bitcast.8), custom_call_target="tpu_custom_call" | custom-call | tf_op jit(solution)/shard_map/finish/pallas_call | solution.py:564
  105.3 0.6 copy.14

commit v4 on v3

--- a/solution.py
+++ b/solution.py
@@ -280,12 +280,12 @@
 
         lax.fori_loop(0, CX, body, 0)
         if not last:
-            if send:
-                send_y(n + 1, c)
             if c == 0:
                 send_x(n + 1, 0)
             if c == CHUNKS - 1:
                 send_x(n + 1, 1)
+            if send:
+                send_y(n + 1, c)
         else:
             save(c).start()
 

time: 106 us -> 107 us (level)
  no operation moved by 1% of the time
where the time goes in v4:
time: 107 us; the launch traced here: 106 us
  Pallas kernels  105 us (98%)
    pallas_call x1, Pallas kernels, body(): pl.pallas_call(kernel, out_shape=(jax.ShapeDtypeStruct(field, F32), jax.S...  103 us
    pallas_call x1, Pallas kernels, body(): pl.pallas_call(finish, out_shape=(jax.ShapeDtypeStruct(field, F32),) * 2,...  2.43 us

profile of v4, /device:TPU:1, one launch (start us, length us, event | category | flops | bytes accessed | tf_op | source)
XLA Modules:
  0.0 106.4 jit_solution(1551549294931771401)
XLA Ops:
  0.6 102.6 %flow_tucker.1 = (f32[16,16,8,128]{3,2,1,0:T(8,128)S(1)}, f32[16,16,8,128]{3,2,1,0:T(8,128)S(1)}, f32[8,16,8,128]{3,2,1,0:T(8,128)S(1)}, f32[8,8,32]{2,1,0:T(8,128)S(1)}) custom-call(f32[16,16,8,128]{3,2,1,0:T(8,128)} %v_hbm.1, f32[3,16,8,128]{3,2,1,0:T(8,128)} %flow_hbm.1, f32[16,8,128]{2,1,0:T(8,128)} %temp_hbm.1, f32[16]{0:T(128)} %diff_ref.1, ...), custom_call_target="tpu_custom_call" | custom-call | tf_op jit(solution)/shard_map/flow_tucker/pallas_call | solution.py:521
  103.3 2.4 %finish.1 = (f32[16,16,8,128]{3,2,1,0:T(8,128)}, f32[16,16,8,128]{3,2,1,0:T(8,128)}) custom-call(f32[16,16,8,128]{3,2,1,0:T(8,128)S(1)} %get-tuple-element.9.final_ref, f32[16,16,8,128]{3,2,1,0:T(8,128)S(1)} %get-tuple-element.10.snap_ref, f32[8,16,8,128]{3,2,1,0:T(8,128)S(1)} %get-tuple-element.11.rec_ref, f32[8,16]{1,0:T(8,128)} %bitcast.8), custom_call_target="tpu_custom_call" | custom-call | tf_op jit(solution)/shard_map/finish/pallas_call | solution.py:564
  105.7 0.6 copy.14
